TPU v7x, 256 devices: a whole 4x4x8 slice. The times are simulated.
256 devices in a mesh: sub: 256 (over z, y, x, core).
Axes of the slice: x: 4, y: 4, z: 8, core: 2. Of those that a mesh axis runs over, the one named last changes fastest.
Arguments:
- stiffness: float32 [256, 1024, 1024], P('sub'), as said below
- neumann_inv: float32 [256, 1024, 1024], P('sub'), as said below
- coarse_basis: float32 [256, 16, 1024], P('sub'), may hold values from -0.375 to 0.375
- coarse_inv: float32 [4096, 4096], P('sub'), as said below
- loads: float32 [256, 64, 1024], P('sub'), may hold values from -6 to 6
- face_index: int32 [256, 4, 128], P('sub'), may hold values from 0 to 1023, as said below
- face_len: int32 [256, 4], P('sub'), may hold values from 0 to 128, as said below
Outputs:
- solution: float32 [256, 64, 1024], P('sub')
- residual: float32 [256, 64, 1024], P('sub')
Inputs may be any that keep to these rules, and one draw needn't show every extreme that they name: `face_index`: within one subdomain all 512 entries are distinct. `face_len`: A block without a neighbour has length 0; paired blocks of two neighbours have equal length; some block has length 128. `stiffness`: each matrix is exactly symmetric and positive definite. `neumann_inv`: each matrix is exactly symmetric and positive definite. `coarse_inv`: the matrix is exactly symmetric and positive definite.
All inputs are finite; a program needn't handle non-finite values.
Results may differ from a plain program's by a relative error of at most 0.00022.
Values sent between devices are 32-bit elements; how exact they have to be, the bound alone decides.
A program may use at most 64 MiB of HBM per device.

v0:
```python
import jax
import jax.numpy as jnp
from jax import lax
from jax.sharding import PartitionSpec as P

CYCLE = 16
ITERS = 4
HIGH = lax.Precision.HIGHEST


def from_behind(value, axis, by):
    length = lax.axis_size(axis)
    pairs = [(i, i + by) for i in range(length) if 0 <= i + by < length]
    return lax.ppermute(value, axis, pairs)


def local(stiffness, neumann_inv, coarse_basis, coarse_inv, loads, face_index, face_len):
    stiff = stiffness[0]
    local_inv = neumann_inv[0]
    basis = coarse_basis[0]
    width = face_index.shape[2]
    face_slots = face_index[0].reshape(-1)
    slot_pos = jnp.arange(width, dtype=jnp.int32)
    live_slots = (slot_pos[None, :] < face_len[0][:, None]).astype(jnp.float32).reshape(-1)
    counts = jnp.ones((stiff.shape[0],), jnp.float32).at[face_slots].add(live_slots)
    weight = 1.0 / counts

    def assemble(local_vals):
        cases = local_vals.shape[0]
        face_vals = jnp.take(local_vals, face_slots, axis=1) * live_slots[None, :]
        blocks = face_vals.reshape(cases, 4, width)
        west_in = from_behind(blocks[:, 1], "sub", 1)
        east_in = from_behind(blocks[:, 0], "sub", -1)
        south_in = from_behind(blocks[:, 3], "sub", CYCLE)
        north_in = from_behind(blocks[:, 2], "sub", -CYCLE)
        incoming = jnp.stack([west_in, east_in, south_in, north_in], axis=1).reshape(cases, -1)
        incoming = incoming * live_slots[None, :]
        return local_vals.at[:, face_slots].add(incoming)

    def inner(left, right):
        return jnp.sum(left * right * weight[None, :], axis=1)

    def coarse_solve(coarse_res):
        return jnp.dot(
            coarse_inv, lax.all_gather(coarse_res, "sub", axis=0, tiled=True), precision=HIGH
        )

    def precond(resid):
        scaled = weight[None, :] * resid
        local_sol = jnp.dot(scaled, local_inv, precision=HIGH)
        coarse_res = jnp.einsum("cn,kn->ck", basis, scaled, precision=HIGH)
        coarse_sol = coarse_solve(coarse_res)
        local_sol = local_sol + jnp.einsum("ck,cn->kn", coarse_sol, basis, precision=HIGH)
        return assemble(weight[None, :] * local_sol)

    def progress_sum(resid, precond_res):
        return lax.psum(inner(resid, precond_res), "sub")

    residual = assemble(loads[0])
    solution = jnp.zeros_like(residual)
    precond_res = precond(residual)
    direction = precond_res
    rz_now = progress_sum(residual, precond_res)
    for step in range(ITERS):
        image = assemble(jnp.dot(direction, stiff, precision=HIGH))
        alpha = rz_now / lax.psum(inner(direction, image), "sub")
        solution = solution + alpha[:, None] * direction
        residual = residual - alpha[:, None] * image
        if step + 1 < ITERS:
            precond_res = precond(residual)
            rz_next = progress_sum(residual, precond_res)
            direction = precond_res + (rz_next / rz_now)[:, None] * direction
            rz_now = rz_next
    return (solution[None], residual[None])


def solution(mesh):
    placed = (
        P("sub", None, None),
        P("sub", None, None),
        P("sub", None, None),
        P("sub", None),
        P("sub", None, None),
        P("sub", None, None),
        P("sub", None),
    )
    return jax.shard_map(
        local,
        mesh=mesh,
        in_specs=placed,
        out_specs=(P("sub", None, None), P("sub", None, None)),
        check_vma=False,
    )
```

profile of v0, /device:TPU:1, one launch (start us, length us, event | category | flops | bytes accessed | tf_op | source)
XLA Modules:
  0.0 1297.2 jit_solution(2350251910647447329)
XLA Ops:
  11.8 4.5 collective-permute-start
  17.6 5.5 collective-permute-start.2
  26.3 4.1 scatter_custom_fusion.1
  30.6 3.5 scatter_custom_fusion
  35.3 111.1 %all-gather.5.cloned.1.call-done = f32[4096,64]{1,0:T(8,128)} async-done(((f32[16,64]{1,0:T(8,128)}), f32[4096,64]{1,0:T(8,128)}) %all-gather.5.cloned.1.call-update) | async-done | bytes 1048592 | tf_op jit(solution)/shard_map/all_gather | solution.py:45
  146.4 5.0 fusion.88
  151.8 4.8 fusion.19
  162.7 5.5 collective-permute-start.6
  170.1 3.6 collective-permute-done.5
  173.9 4.0 scatter_custom_fusion.2
  177.9 8.5 fusion.6
  190.9 6.0 collective-permute-start.10
  202.9 3.5 scatter_custom_fusion.3
  206.8 90.3 %all-reduce = (f32[64]{0:T(128)S(1)}, f32[64]{0:T(128)S(1)}) all-reduce(f32[64]{0:T(128)S(1)} %get-tuple-element.4, f32[64]{0:T(128)S(1)} %get-tuple-element.3), channel_id=1, replica_groups=mesh['sub'=256] {'sub'}, use_global_device_ids=true, to_apply=%region_4.6 | all-reduce | flops 128 | bytes 1024 | tf_op jit(solution)/shard_map/psum | solution.py:57
  298.4 100.4 %all-gather.7.cloned.1.call-done = f32[4096,64]{1,0:T(8,128)} async-done(((f32[16,64]{1,0:T(8,128)}), f32[4096,64]{1,0:T(8,128)}) %all-gather.7.cloned.1.call-update) | async-done | bytes 1048592 | tf_op jit(solution)/shard_map/all_gather | solution.py:45
  398.8 5.0 fusion.89
  404.1 4.8 fusion.25
  415.0 5.5 collective-permute-start.14
  422.5 3.6 collective-permute-done.13
  426.3 3.5 scatter_custom_fusion.4
  430.1 83.8 %psum.58 = f32[64]{0:T(128)S(1)} all-reduce(f32[64]{0:T(128)S(1)} %multiply_reduce_fusion.5), channel_id=1, replica_groups=mesh['sub'=256] {'sub'}, use_global_device_ids=true, to_apply=%region_10.12 | all-reduce | flops 64 | bytes 512 | tf_op jit(solution)/shard_map/psum | solution.py:57
  514.0 8.5 fusion.4
  527.0 5.5 collective-permute-start.18
  538.3 3.5 scatter_custom_fusion.5
  542.1 85.6 %psum.59 = f32[64]{0:T(128)S(1)} all-reduce(f32[64]{0:T(128)S(1)} %multiply_reduce_fusion.4), channel_id=1, replica_groups=mesh['sub'=256] {'sub'}, use_global_device_ids=true, to_apply=%region_13.15 | all-reduce | flops 64 | bytes 512 | tf_op jit(solution)/shard_map/psum | solution.py:66
  629.1 100.3 %all-gather.9.cloned.1.call-done = f32[4096,64]{1,0:T(8,128)} async-done(((f32[16,64]{1,0:T(8,128)}), f32[4096,64]{1,0:T(8,128)}) %all-gather.9.cloned.1.call-update) | async-done | bytes 1048592 | tf_op jit(solution)/shard_map/all_gather | solution.py:45
  729.4 5.0 fusion.90
  734.8 4.8 fusion.31
  741.1 3.2 collective-permute-start.20
  745.7 5.5 collective-permute-start.22
  753.1 3.6 collective-permute-done.21
  756.9 3.5 scatter_custom_fusion.6
  760.8 84.0 %psum.60 = f32[64]{0:T(128)S(1)} all-reduce(f32[64]{0:T(128)S(1)} %multiply_reduce_fusion.3), channel_id=1, replica_groups=mesh['sub'=256] {'sub'}, use_global_device_ids=true, to_apply=%region_16.18 | all-reduce | flops 64 | bytes 512 | tf_op jit(solution)/shard_map/psum | solution.py:57
  844.9 8.5 fusion.2
  857.9 5.5 collective-permute-start.26
  869.1 3.5 scatter_custom_fusion.7
  873.0 85.8 %psum.61 = f32[64]{0:T(128)S(1)} all-reduce(f32[64]{0:T(128)S(1)} %multiply_reduce_fusion.2), channel_id=1, replica_groups=mesh['sub'=256] {'sub'}, use_global_device_ids=true, to_apply=%region_19.21 | all-reduce | flops 64 | bytes 512 | tf_op jit(solution)/shard_map/psum | solution.py:66
  959.8 100.6 %all-gather.11.cloned.1.call-done = f32[4096,64]{1,0:T(8,128)} async-done(((f32[16,64]{1,0:T(8,128)}), f32[4096,64]{1,0:T(8,128)}) %all-gather.11.cloned.1.call-update) | async-done | bytes 1048592 | tf_op jit(solution)/shard_map/all_gather | solution.py:45
  1060.5 5.0 fusion.91
  1065.8 4.8 fusion.37
  1076.7 5.5 collective-permute-start.30
  1084.2 3.6 collective-permute-done.29
  1087.9 3.5 scatter_custom_fusion.8
  1091.8 83.8 %psum.62 = f32[64]{0:T(128)S(1)} all-reduce(f32[64]{0:T(128)S(1)} %multiply_reduce_fusion.1), channel_id=1, replica_groups=mesh['sub'=256] {'sub'}, use_global_device_ids=true, to_apply=%region_22.24 | all-reduce | flops 64 | bytes 512 | tf_op jit(solution)/shard_map/psum | solution.py:57
  1175.6 8.5 fusion
  1188.6 5.5 collective-permute-start.34
  1199.9 3.5 scatter_custom_fusion.9
  1203.8 85.6 %psum.63 = f32[64]{0:T(128)S(1)} all-reduce(f32[64]{0:T(128)S(1)} %multiply_reduce_fusion), channel_id=1, replica_groups=mesh['sub'=256] {'sub'}, use_global_device_ids=true, to_apply=%region_25.27 | all-reduce | flops 64 | bytes 512 | tf_op jit(solution)/shard_map/psum | solution.py:66
  (162 shorter events, 88.8 us)
Async XLA Ops:
  7.2 139.3 %copy-start = (f32[16,4096]{1,0:T(8,128)S(1)}, f32[16,4096]{1,0:T(8,128)}, u32[]{:S(2)}) copy-start(f32[16,4096]{1,0:T(8,128)} %param.12) | copy-start | bytes 786436
  7.2 27.1 %copy-start.1 = (f32[1,16,1024]{2,1,0:T(8,128)S(1)}, f32[1,16,1024]{2,1,0:T(8,128)}, u32[]{:S(2)}) copy-start(f32[1,16,1024]{2,1,0:T(8,128)} %param.11) | copy-start | bytes 196612
  7.2 139.2 %all-gather.5.cloned.1.call-start = ((), (), s32[]{:S(2)}) async-start(), calls=%async_computation | async-start | bytes 2105344 | tf_op jit(solution)/shard_map/all_gather | solution.py:45
  11.8 18.6 %collective-permute-start = (f32[64,128]{0,1:T(8,128)S(1)}, f32[64,128]{0,1:T(8,128)S(1)}, u32[]{:S(2)}, u32[]{:S(2)}) collective-permute-start(f32[64,128]{0,1:T(8,128)S(1)} %get-tuple-element.39), channel_id=1, source_target_pairs={{0,1},{1,2},{2,3},{3,4},{4,5},{5,6},{6,7},{7,8},{8,9},{9,10},{10,1... | collective-permute-start | bytes 98312 | tf_op jit(solution)/shard_map/ppermute | solution.py:14
  16.3 14.1 %collective-permute-start.3 = (f32[64,128]{0,1:T(8,128)S(1)}, f32[64,128]{0,1:T(8,128)S(1)}, u32[]{:S(2)}, u32[]{:S(2)}) collective-permute-start(f32[64,128]{0,1:T(8,128)S(1)} %get-tuple-element.40), channel_id=1, source_target_pairs={{16,0},{17,1},{18,2},{19,3},{20,4},{21,5},{22,6},{23,7},{24,8},{25... | collective-permute-start | bytes 98312 | tf_op jit(solution)/shard_map/ppermute | solution.py:14
  17.6 12.8 collective-permute-start.2
  23.1 7.3 collective-permute-start.1
  35.3 363.5 %all-gather.7.cloned.1.call-start = ((), (), s32[]{:S(2)}) async-start(), calls=%async_computation.1 | async-start | bytes 2105344 | tf_op jit(solution)/shard_map/all_gather | solution.py:45
  158.1 12.0 collective-permute-start.4
  161.4 8.7 collective-permute-start.7
  162.7 7.5 collective-permute-start.6
  168.2 5.6 collective-permute-start.5
  187.7 12.2 collective-permute-start.8
  189.6 10.3 collective-permute-start.11
  190.9 9.0 collective-permute-start.10
  197.0 5.8 collective-permute-start.9
  298.2 431.2 %all-gather.9.cloned.1.call-start = ((), (), s32[]{:S(2)}) async-start(), calls=%async_computation.2 | async-start | bytes 2105344 | tf_op jit(solution)/shard_map/all_gather | solution.py:45
  410.5 12.0 collective-permute-start.12
  413.7 8.7 collective-permute-start.15
  415.0 7.5 collective-permute-start.14
  420.5 5.6 collective-permute-start.13
  523.8 11.7 collective-permute-start.16
  525.7 9.8 collective-permute-start.19
  527.0 8.5 collective-permute-start.18
  532.5 5.6 collective-permute-start.17
  628.8 431.6 %all-gather.11.cloned.1.call-start = ((), (), s32[]{:S(2)}) async-start(), calls=%async_computation.3 | async-start | bytes 2105344 | tf_op jit(solution)/shard_map/all_gather | solution.py:45
  741.1 12.0 collective-permute-start.20
  744.4 8.7 collective-permute-start.23
  745.7 7.5 collective-permute-start.22
  751.2 5.6 collective-permute-start.21
  854.7 11.7 collective-permute-start.24
  856.6 9.8 collective-permute-start.27
  857.9 8.5 collective-permute-start.26
  863.4 5.6 collective-permute-start.25
  1072.1 12.0 collective-permute-start.28
  1075.4 8.7 collective-permute-start.31
  1076.7 7.5 collective-permute-start.30
  1082.2 5.6 collective-permute-start.29
  1185.4 11.7 collective-permute-start.32
  1187.3 9.8 collective-permute-start.35
  1188.6 8.5 collective-permute-start.34
  1194.1 5.6 collective-permute-start.33
Sparse Core Ops, SparseCore 0:
  35.4 110.9 all-gather.4
  298.3 100.4 all-gather.6
  628.9 100.4 all-gather.8
  960.0 100.4 all-gather.10
where the time goes:
time: 1310 us; the launch traced here: 1300 us
  blocking collectives  599 us (46%)
  waiting for transfers between devices  438 us (33%)
  starting transfers between devices  109 us (8%)
  matrix products  78.4 us (6%)
  other arithmetic  44.7 us (3%)
  between operations  15.2 us (1%)
  local copies, waits for them, and re-layouts  13.1 us (1%)
    all_gather x4, waiting for transfers between devices, coarse_solve(): lax.all_gather(coarse_res, 'sub', axis=0, tiled=True)  412 us
    psum x4, blocking collectives, progress_sum(): return lax.psum(inner(resid, precond_res), 'sub')  342 us
    psum x3, blocking collectives, local(): alpha = rz_now / lax.psum(inner(direction, image), 'sub')  257 us
    ppermute x36, starting transfers between devices, from_behind(): return lax.ppermute(value, axis, pairs)  109 us
    dot_general x4, matrix products, local(): image = assemble(jnp.dot(direction, stiff, precision=HIGH))  34 us
    scatter-add x9, other arithmetic, assemble(): return local_vals.at[:, face_slots].add(incoming)  32.2 us
  transfers between devices with their start and end apart: 40, of which 12 were waited for; matrix products, arithmetic and copies ran while one was open for 0% of the time, Pallas kernels for 0%

commit v1 on v0

--- a/solution.py
+++ b/solution.py
@@ -6,6 +6,13 @@
 CYCLE = 16
 ITERS = 4
 HIGH = lax.Precision.HIGHEST
+
+
+def all_by_exchange(x, name, along):
+    size = lax.axis_size(name)
+    pieces = jnp.stack([x for _ in range(size)])
+    pieces = lax.all_to_all(pieces, name, split_axis=0, concat_axis=0)
+    return jnp.concatenate(pieces, axis=along)
 
 
 def from_behind(value, axis, by):
@@ -41,9 +48,7 @@
         return jnp.sum(left * right * weight[None, :], axis=1)
 
     def coarse_solve(coarse_res):
-        return jnp.dot(
-            coarse_inv, lax.all_gather(coarse_res, "sub", axis=0, tiled=True), precision=HIGH
-        )
+        return jnp.dot(coarse_inv, all_by_exchange(coarse_res, "sub", 0), precision=HIGH)
 
     def precond(resid):
         scaled = weight[None, :] * resid

time: 1310 us -> 1070 us (0.82)
  waiting for transfers between devices: 438 us -> 24.5 us
  blocking collectives: 599 us -> 762 us
  other arithmetic: 44.7 us -> 62.1 us
  local copies, waits for them, and re-layouts: 13.1 us -> 30.2 us
    all_gather x4 -> x0, waiting for transfers between devices: 412 us -> none  [coarse_solve(): lax.all_gather(coarse_res, 'sub', axis=0, tiled=True)]
    all_to_all x0 -> x4, blocking collectives: none -> 165 us  [all_by_exchange(): pieces = lax.all_to_all(pieces, name, split_axis=0, concat_axis=0)]
    all_to_all x0 -> x4, other arithmetic: none -> 17.4 us  [all_by_exchange(): pieces = lax.all_to_all(pieces, name, split_axis=0, concat_axis=0)]
    unnamed x5 -> x17, local copies, waits for them, and re-layouts: 1.16 us -> 17.1 us
  transfers between devices with their start and end apart: 40 -> 36, of which waited for: 12 -> 8; matrix products, arithmetic and copies ran while one was open for 0% -> 0% of each run, Pallas kernels for 0% -> 0%
where the time goes in v1:
time: 1070 us; the launch traced here: 1060 us
  blocking collectives  762 us (71%)
  starting transfers between devices  110 us (10%)
  matrix products  69.5 us (6%)
  other arithmetic  62.1 us (6%)
  local copies, waits for them, and re-layouts  30.2 us (3%)
  waiting for transfers between devices  24.5 us (2%)
    psum x4, blocking collectives, progress_sum(): return lax.psum(inner(resid, precond_res), 'sub')  340 us
    psum x3, blocking collectives, local(): alpha = rz_now / lax.psum(inner(direction, image), 'sub')  257 us
    all_to_all x4, blocking collectives, all_by_exchange(): pieces = lax.all_to_all(pieces, name, split_axis=0, concat_axis=0)  165 us
    ppermute x36, starting transfers between devices, from_behind(): return lax.ppermute(value, axis, pairs)  110 us
    dot_general x4, matrix products, local(): image = assemble(jnp.dot(direction, stiff, precision=HIGH))  34 us
    scatter-add x9, other arithmetic, assemble(): return local_vals.at[:, face_slots].add(incoming)  32.1 us
    ppermute x36, waiting for transfers between devices, from_behind(): return lax.ppermute(value, axis, pairs)  24.5 us
  transfers between devices with their start and end apart: 36, of which 8 were waited for; matrix products, arithmetic and copies ran while one was open for 0% of the time, Pallas kernels for 0%

profile of v1, /device:TPU:1, one launch (start us, length us, event | category | flops | bytes accessed | tf_op | source)
XLA Modules:
  0.0 1060.0 jit_solution(10309809624951423216)
XLA Ops:
  5.2 4.5 collective-permute-start
  11.1 5.5 collective-permute-start.2
  19.7 4.1 scatter_custom_fusion.1
  24.0 3.5 scatter_custom_fusion
  30.5 49.1 %all_to_all.20 = f32[256,1,1024]{2,1,0:T(1,128)S(1)} all-to-all(f32[256,1,1024]{2,1,0:T(1,128)} %reshape.362), channel_id=1, replica_groups=mesh['sub'=256] {'sub'}, dimensions={0} | all-to-all | bytes 2097152 | tf_op jit(solution)/shard_map/all_to_all | solution.py:14
  80.1 4.3 reduce
  89.9 4.8 fusion.19
  101.0 5.5 collective-permute-start.6
  108.5 3.6 collective-permute-done.5
  112.3 3.9 scatter_custom_fusion.2
  116.2 8.5 fusion.6
  129.2 5.8 collective-permute-start.10
  140.8 3.5 scatter_custom_fusion.3
  144.6 90.2 %all-reduce = (f32[64]{0:T(128)S(1)}, f32[64]{0:T(128)S(1)}) all-reduce(f32[64]{0:T(128)S(1)} %get-tuple-element.4, f32[64]{0:T(128)S(1)} %get-tuple-element.3), channel_id=1, replica_groups=mesh['sub'=256] {'sub'}, use_global_device_ids=true, to_apply=%region_4.6 | all-reduce | flops 128 | bytes 1024 | tf_op jit(solution)/shard_map/psum | solution.py:62
  237.7 38.5 %all_to_all.21 = f32[256,1,1024]{2,1,0:T(1,128)S(1)} all-to-all(f32[256,1,1024]{2,1,0:T(1,128)} %reshape.364), channel_id=1, replica_groups=mesh['sub'=256] {'sub'}, dimensions={0} | all-to-all | bytes 2097152 | tf_op jit(solution)/shard_map/all_to_all | solution.py:14
  276.3 4.4 reduce.1
  286.1 4.8 fusion.25
  292.4 3.5 collective-permute-start.12
  297.2 5.5 collective-permute-start.14
  304.7 3.6 collective-permute-done.13
  308.4 3.5 scatter_custom_fusion.4
  312.3 83.3 %psum.58 = f32[64]{0:T(128)S(1)} all-reduce(f32[64]{0:T(128)S(1)} %multiply_reduce_fusion.5), channel_id=1, replica_groups=mesh['sub'=256] {'sub'}, use_global_device_ids=true, to_apply=%region_10.12 | all-reduce | flops 64 | bytes 512 | tf_op jit(solution)/shard_map/psum | solution.py:62
  395.7 8.5 fusion.4
  408.7 5.5 collective-permute-start.18
  419.9 3.5 scatter_custom_fusion.5
  423.7 85.6 %psum.59 = f32[64]{0:T(128)S(1)} all-reduce(f32[64]{0:T(128)S(1)} %multiply_reduce_fusion.4), channel_id=1, replica_groups=mesh['sub'=256] {'sub'}, use_global_device_ids=true, to_apply=%region_13.15 | all-reduce | flops 64 | bytes 512 | tf_op jit(solution)/shard_map/psum | solution.py:71
  512.2 38.8 %all_to_all.22 = f32[256,1,1024]{2,1,0:T(1,128)S(1)} all-to-all(f32[256,1,1024]{2,1,0:T(1,128)} %reshape.366), channel_id=1, replica_groups=mesh['sub'=256] {'sub'}, dimensions={0} | all-to-all | bytes 2097152 | tf_op jit(solution)/shard_map/all_to_all | solution.py:14
  551.0 4.4 reduce.2
  560.8 4.8 fusion.31
  571.9 5.5 collective-permute-start.22
  579.3 3.6 collective-permute-done.21
  583.1 3.5 scatter_custom_fusion.6
  587.0 83.2 %psum.60 = f32[64]{0:T(128)S(1)} all-reduce(f32[64]{0:T(128)S(1)} %multiply_reduce_fusion.3), channel_id=1, replica_groups=mesh['sub'=256] {'sub'}, use_global_device_ids=true, to_apply=%region_16.18 | all-reduce | flops 64 | bytes 512 | tf_op jit(solution)/shard_map/psum | solution.py:62
  670.3 8.5 fusion.2
  683.3 5.5 collective-permute-start.26
  694.6 3.5 scatter_custom_fusion.7
  698.4 85.6 %psum.61 = f32[64]{0:T(128)S(1)} all-reduce(f32[64]{0:T(128)S(1)} %multiply_reduce_fusion.2), channel_id=1, replica_groups=mesh['sub'=256] {'sub'}, use_global_device_ids=true, to_apply=%region_19.21 | all-reduce | flops 64 | bytes 512 | tf_op jit(solution)/shard_map/psum | solution.py:71
  786.9 38.6 %all_to_all.23 = f32[256,1,1024]{2,1,0:T(1,128)S(1)} all-to-all(f32[256,1,1024]{2,1,0:T(1,128)} %reshape.368), channel_id=1, replica_groups=mesh['sub'=256] {'sub'}, dimensions={0} | all-to-all | bytes 2097152 | tf_op jit(solution)/shard_map/all_to_all | solution.py:14
  825.4 4.4 reduce.3
  835.3 4.8 fusion.37
  846.4 5.5 collective-permute-start.30
  853.8 3.6 collective-permute-done.29
  857.6 3.5 scatter_custom_fusion.8
  861.4 83.3 %psum.62 = f32[64]{0:T(128)S(1)} all-reduce(f32[64]{0:T(128)S(1)} %multiply_reduce_fusion.1), channel_id=1, replica_groups=mesh['sub'=256] {'sub'}, use_global_device_ids=true, to_apply=%region_22.24 | all-reduce | flops 64 | bytes 512 | tf_op jit(solution)/shard_map/psum | solution.py:62
  944.8 8.6 fusion
  957.9 5.5 collective-permute-start.34
  969.1 3.5 scatter_custom_fusion.9
  973.0 85.6 %psum.63 = f32[64]{0:T(128)S(1)} all-reduce(f32[64]{0:T(128)S(1)} %multiply_reduce_fusion), channel_id=1, replica_groups=mesh['sub'=256] {'sub'}, use_global_device_ids=true, to_apply=%region_25.27 | all-reduce | flops 64 | bytes 512 | tf_op jit(solution)/shard_map/psum | solution.py:71
  (175 shorter events, 116.9 us)
Async XLA Ops:
  0.6 85.5 %copy-start = (f32[16,4096]{1,0:T(8,128)S(1)}, f32[16,4096]{1,0:T(8,128)}, u32[]{:S(2)}) copy-start(f32[16,4096]{1,0:T(8,128)} %param.12) | copy-start | bytes 786436
  0.6 27.1 %copy-start.3 = (f32[1,16,1024]{2,1,0:T(8,128)S(1)}, f32[1,16,1024]{2,1,0:T(8,128)}, u32[]{:S(2)}) copy-start(f32[1,16,1024]{2,1,0:T(8,128)} %param.11) | copy-start | bytes 196612
  5.2 18.6 %collective-permute-start = (f32[64,128]{0,1:T(8,128)S(1)}, f32[64,128]{0,1:T(8,128)S(1)}, u32[]{:S(2)}, u32[]{:S(2)}) collective-permute-start(f32[64,128]{0,1:T(8,128)S(1)} %get-tuple-element.39), channel_id=1, source_target_pairs={{0,1},{1,2},{2,3},{3,4},{4,5},{5,6},{6,7},{7,8},{8,9},{9,10},{10,1... | collective-permute-start | bytes 98312 | tf_op jit(solution)/shard_map/ppermute | solution.py:21
  9.8 14.1 %collective-permute-start.3 = (f32[64,128]{0,1:T(8,128)S(1)}, f32[64,128]{0,1:T(8,128)S(1)}, u32[]{:S(2)}, u32[]{:S(2)}) collective-permute-start(f32[64,128]{0,1:T(8,128)S(1)} %get-tuple-element.40), channel_id=1, source_target_pairs={{16,0},{17,1},{18,2},{19,3},{20,4},{21,5},{22,6},{23,7},{24,8},{25... | collective-permute-start | bytes 98312 | tf_op jit(solution)/shard_map/ppermute | solution.py:21
  11.1 12.8 %collective-permute-start.2 = (f32[64,128]{0,1:T(8,128)S(1)}, f32[64,128]{0,1:T(8,128)S(1)}, u32[]{:S(2)}, u32[]{:S(2)}) collective-permute-start(f32[64,128]{0,1:T(8,128)S(1)} %get-tuple-element.41), channel_id=1, source_target_pairs={{0,16},{1,17},{2,18},{3,19},{4,20},{5,21},{6,22},{7,23},{8,24},{9,... | collective-permute-start | bytes 98312 | tf_op jit(solution)/shard_map/ppermute | solution.py:21
  16.6 7.3 collective-permute-start.1
  96.3 12.2 %collective-permute-start.4 = (f32[64,128]{0,1:T(8,128)S(1)}, f32[64,128]{0,1:T(8,128)S(1)}, u32[]{:S(2)}, u32[]{:S(2)}) collective-permute-start(f32[64,128]{0,1:T(8,128)S(1)} %get-tuple-element.35), channel_id=1, source_target_pairs={{0,1},{1,2},{2,3},{3,4},{4,5},{5,6},{6,7},{7,8},{8,9},{9,10},{10,1... | collective-permute-start | bytes 98312 | tf_op jit(solution)/shard_map/ppermute | solution.py:21
  99.7 8.7 collective-permute-start.7
  101.0 7.5 collective-permute-start.6
  106.5 5.6 collective-permute-start.5
  126.0 12.4 %collective-permute-start.8 = (f32[64,128]{0,1:T(8,128)S(1)}, f32[64,128]{0,1:T(8,128)S(1)}, u32[]{:S(2)}, u32[]{:S(2)}) collective-permute-start(f32[64,128]{0,1:T(8,128)S(1)} %get-tuple-element.31), channel_id=1, source_target_pairs={{0,1},{1,2},{2,3},{3,4},{4,5},{5,6},{6,7},{7,8},{8,9},{9,10},{10,1... | collective-permute-start | bytes 98312 | tf_op jit(solution)/shard_map/ppermute | solution.py:21
  127.9 10.5 collective-permute-start.11
  129.2 9.2 collective-permute-start.10
  135.0 5.6 collective-permute-start.9
  138.3 257.2 %copy-start.1 = (f32[64,1024]{1,0:T(8,128)}, f32[64,1024]{1,0:T(8,128)S(1)}, u32[]{:S(2)}) copy-start(f32[64,1024]{1,0:T(8,128)S(1)} %copy.14) | copy-start | bytes 786436
  292.4 12.2 %collective-permute-start.12 = (f32[64,128]{0,1:T(8,128)S(1)}, f32[64,128]{0,1:T(8,128)S(1)}, u32[]{:S(2)}, u32[]{:S(2)}) collective-permute-start(f32[64,128]{0,1:T(8,128)S(1)} %get-tuple-element.27), channel_id=1, source_target_pairs={{0,1},{1,2},{2,3},{3,4},{4,5},{5,6},{6,7},{7,8},{8,9},{9,10},{10,1... | collective-permute-start | bytes 98312 | tf_op jit(solution)/shard_map/ppermute | solution.py:21
  295.9 8.7 collective-permute-start.15
  297.2 7.5 collective-permute-start.14
  302.7 5.6 collective-permute-start.13
  405.4 11.7 %collective-permute-start.16 = (f32[64,128]{0,1:T(8,128)S(1)}, f32[64,128]{0,1:T(8,128)S(1)}, u32[]{:S(2)}, u32[]{:S(2)}) collective-permute-start(f32[64,128]{0,1:T(8,128)S(1)} %get-tuple-element.23), channel_id=1, source_target_pairs={{0,1},{1,2},{2,3},{3,4},{4,5},{5,6},{6,7},{7,8},{8,9},{9,10},{10,1... | collective-permute-start | bytes 98312 | tf_op jit(solution)/shard_map/ppermute | solution.py:21
  407.4 9.8 collective-permute-start.19
  408.7 8.5 collective-permute-start.18
  414.2 5.6 collective-permute-start.17
  567.1 12.2 %collective-permute-start.20 = (f32[64,128]{0,1:T(8,128)S(1)}, f32[64,128]{0,1:T(8,128)S(1)}, u32[]{:S(2)}, u32[]{:S(2)}) collective-permute-start(f32[64,128]{0,1:T(8,128)S(1)} %get-tuple-element.19), channel_id=1, source_target_pairs={{0,1},{1,2},{2,3},{3,4},{4,5},{5,6},{6,7},{7,8},{8,9},{9,10},{10,1... | collective-permute-start | bytes 98312 | tf_op jit(solution)/shard_map/ppermute | solution.py:21
  570.6 8.7 collective-permute-start.23
  571.9 7.5 collective-permute-start.22
  577.4 5.6 collective-permute-start.21
  680.1 11.7 %collective-permute-start.24 = (f32[64,128]{0,1:T(8,128)S(1)}, f32[64,128]{0,1:T(8,128)S(1)}, u32[]{:S(2)}, u32[]{:S(2)}) collective-permute-start(f32[64,128]{0,1:T(8,128)S(1)} %get-tuple-element.15), channel_id=1, source_target_pairs={{0,1},{1,2},{2,3},{3,4},{4,5},{5,6},{6,7},{7,8},{8,9},{9,10},{10,1... | collective-permute-start | bytes 98312 | tf_op jit(solution)/shard_map/ppermute | solution.py:21
  682.0 9.8 collective-permute-start.27
  683.3 8.5 collective-permute-start.26
  688.8 5.6 collective-permute-start.25
  841.6 12.2 %collective-permute-start.28 = (f32[64,128]{0,1:T(8,128)S(1)}, f32[64,128]{0,1:T(8,128)S(1)}, u32[]{:S(2)}, u32[]{:S(2)}) collective-permute-start(f32[64,128]{0,1:T(8,128)S(1)} %get-tuple-element.11), channel_id=1, source_target_pairs={{0,1},{1,2},{2,3},{3,4},{4,5},{5,6},{6,7},{7,8},{8,9},{9,10},{10,1... | collective-permute-start | bytes 98312 | tf_op jit(solution)/shard_map/ppermute | solution.py:21
  845.1 8.7 collective-permute-start.31
  846.4 7.5 collective-permute-start.30
  851.9 5.6 collective-permute-start.29
  944.8 113.9 %copy-start.2 = (f32[64,1024]{1,0:T(8,128)S(1)}, f32[64,1024]{1,0:T(8,128)}, u32[]{:S(2)}) copy-start(f32[64,1024]{1,0:T(8,128)} %copy-done.1) | copy-start | bytes 786436
  954.6 11.7 %collective-permute-start.32 = (f32[64,128]{0,1:T(8,128)S(1)}, f32[64,128]{0,1:T(8,128)S(1)}, u32[]{:S(2)}, u32[]{:S(2)}) collective-permute-start(f32[64,128]{0,1:T(8,128)S(1)} %get-tuple-element.7), channel_id=1, source_target_pairs={{0,1},{1,2},{2,3},{3,4},{4,5},{5,6},{6,7},{7,8},{8,9},{9,10},{10,1... | collective-permute-start | bytes 98312 | tf_op jit(solution)/shard_map/ppermute | solution.py:21
  956.6 9.8 collective-permute-start.35
  957.9 8.5 collective-permute-start.34
  963.4 5.6 collective-permute-start.33
